TPU v7x, 128 devices: a whole 4x4x4 slice. The times are simulated.
128 devices in a mesh: tok: 32 (over y, x, core), head: 4 (over z).
Axes of the slice: x: 4, y: 4, z: 4, core: 2. Of those that a mesh axis runs over, the one named last changes fastest.
Arguments:
- layer_input: bfloat16 [16384, 5120], P('tok', 'head'), may hold values from -6 to 6
- rate_weight: bfloat16 [5120, 12], P('head'), may hold values from -0.078125 to 0.078125
- token_queries: bfloat16 [16384, 3072], P('tok', 'head'), may hold values from -80 to 80
- token_keys: bfloat16 [16384, 3072], P('tok', 'head'), may hold values from -5 to 5
- token_values: bfloat16 [16384, 3072], P('tok', 'head'), may hold values from -6 to 6
- first_weight: float32 [12, 256, 512], P('head'), may hold values from -0.375 to 0.375
- third_weight: float32 [12, 256, 512], P('head'), may hold values from -0.375 to 0.375
- second_weight: float32 [12, 512, 256], P('head'), may hold values from -0.25 to 0.25
- update_scale: float32 [12], P('head'), may hold values from 0.5 to 2
- out_gain: float32 [3072], P('head'), may hold values from 0.25 to 1.75
Outputs:
- mixed: bfloat16 [16384, 3072], P('tok', 'head')
All inputs are finite; a program needn't handle non-finite values.
Results may differ from a plain program's by a relative error of at most 0.033.
Values may be sent and summed in bfloat16 or wider, within the bound.
A program may use at most 128 MiB of HBM per device.

v0:
```python
import jax
import jax.numpy as jnp
from jax import lax
from jax.sharding import PartitionSpec as P

HDIM = 256
WINDOW = 256
STEPS = 5


COEF_A = 3.4445
COEF_B = -4.775
COEF_C = 2.0315
EPS_SCALE = 1e-07
EPS_RMS = 1e-06


def passed_along(block, axis, distance):
    devices = range(lax.axis_size(axis))
    route = [(i - distance, i) for i in devices if i - distance in devices]
    return lax.ppermute(block, axis, route)


def head_gradients(key_three, value_three, token_rates, first_weight, third_weight, second_weight):
    first_half = first_weight.astype(jnp.bfloat16)
    third_half = third_weight.astype(jnp.bfloat16)
    second_half = second_weight.astype(jnp.bfloat16)
    gate_pre = jnp.einsum("thd,hdf->thf", key_three, first_half, preferred_element_type=jnp.float32)
    up_pre = jnp.einsum("thd,hdf->thf", key_three, third_half, preferred_element_type=jnp.float32)
    sigmoid_gate = jax.nn.sigmoid(gate_pre)
    activated = gate_pre * sigmoid_gate
    hidden = (activated * up_pre).astype(jnp.bfloat16)
    weighted = (value_three.astype(jnp.float32) * token_rates[:, :, None]).astype(jnp.bfloat16)
    hidden_grad = -jnp.einsum(
        "the,hfe->thf", weighted, second_half, preferred_element_type=jnp.float32
    )
    gate_grad = (
        hidden_grad * up_pre * sigmoid_gate * (1.0 + gate_pre * (1.0 - sigmoid_gate))
    ).astype(jnp.bfloat16)
    up_grad = (hidden_grad * activated).astype(jnp.bfloat16)
    first_grad = jnp.einsum(
        "thd,thf->hdf", key_three, gate_grad, preferred_element_type=jnp.float32
    )
    third_grad = jnp.einsum("thd,thf->hdf", key_three, up_grad, preferred_element_type=jnp.float32)
    second_grad = -jnp.einsum("the,thf->hef", weighted, hidden, preferred_element_type=jnp.float32)
    return jnp.concatenate([first_grad, third_grad, second_grad], axis=0)


def polish(iterate):
    gram_half = jnp.einsum(
        "mik,mjk->mij", iterate, iterate, preferred_element_type=jnp.float32
    ).astype(jnp.bfloat16)
    squared = jnp.einsum("mij,mjk->mik", gram_half, gram_half, preferred_element_type=jnp.float32)
    mixing = (COEF_B * gram_half.astype(jnp.float32) + COEF_C * squared).astype(jnp.bfloat16)
    moved = jnp.einsum("mij,mjk->mik", mixing, iterate, preferred_element_type=jnp.float32)
    return (COEF_A * iterate.astype(jnp.float32) + moved).astype(jnp.bfloat16)


def attend_block(query_block, key_block, value_block, query_place, key_place):
    scores = jnp.einsum(
        "qhd,khd->hqk", query_block, key_block, preferred_element_type=jnp.float32
    ) * HDIM ** (-0.5)
    allowed = (
        (key_place[None, :] <= query_place[:, None])
        & (key_place[None, :] > query_place[:, None] - WINDOW)
        & (key_place[None, :] >= 0)
    )
    scores = jnp.where(allowed[None], scores, -1e30)
    highest = jnp.max(scores, axis=-1, keepdims=True)
    weights = jnp.exp(scores - highest)
    shares = (weights / jnp.sum(weights, axis=-1, keepdims=True)).astype(jnp.bfloat16)
    return jnp.einsum("hqk,khd->qhd", shares, value_block, preferred_element_type=jnp.float32)


def on_device(
    layer_input,
    rate_weight,
    token_queries,
    token_keys,
    token_values,
    first_weight,
    third_weight,
    second_weight,
    update_scale,
    out_gain,
):
    local_rows = token_queries.shape[0]
    local_heads = token_queries.shape[1] // HDIM
    partial_logits = jnp.dot(layer_input, rate_weight, preferred_element_type=jnp.float32)
    token_rates = jax.nn.softplus(
        lax.psum_scatter(partial_logits, "head", scatter_dimension=1, tiled=True)
    )
    query_three = token_queries.reshape(local_rows, local_heads, HDIM)
    key_three = token_keys.reshape(local_rows, local_heads, HDIM)
    value_three = token_values.reshape(local_rows, local_heads, HDIM)
    window_tail = jnp.stack(
        [token_keys[local_rows - WINDOW :], token_values[local_rows - WINDOW :]]
    )
    previous = passed_along(window_tail, "tok", 1)
    stacked = head_gradients(
        key_three, value_three, token_rates, first_weight, third_weight, second_weight
    )
    summed = lax.psum(stacked, "tok")
    squares = jnp.sum(summed * summed, axis=(1, 2))
    iterate = (summed / (jnp.sqrt(squares)[:, None, None] + EPS_SCALE)).astype(jnp.bfloat16)
    for repeat in range(STEPS):
        iterate = polish(iterate)
    ortho_wide = iterate.astype(jnp.float32)
    step_size = update_scale[:, None, None]
    new_first = (first_weight - step_size * ortho_wide[:local_heads]).astype(jnp.bfloat16)
    new_third = (third_weight - step_size * ortho_wide[local_heads : 2 * local_heads]).astype(
        jnp.bfloat16
    )
    new_second = (
        second_weight - step_size * jnp.swapaxes(ortho_wide[2 * local_heads :], 1, 2)
    ).astype(jnp.bfloat16)
    gate_pre = jnp.einsum(
        "thd,hdf->thf", query_three, new_first, preferred_element_type=jnp.float32
    )
    up_pre = jnp.einsum("thd,hdf->thf", query_three, new_third, preferred_element_type=jnp.float32)
    fast_hidden = (gate_pre * jax.nn.sigmoid(gate_pre) * up_pre).astype(jnp.bfloat16)
    fast_out = jnp.einsum(
        "thf,hfe->the", fast_hidden, new_second, preferred_element_type=jnp.float32
    )
    normed = (
        fast_out
        * lax.rsqrt(jnp.mean(fast_out * fast_out, axis=-1, keepdims=True) + EPS_RMS)
        * out_gain.reshape(local_heads, HDIM)
    )
    long_keys = jnp.concatenate([previous[0], token_keys]).reshape(
        local_rows + WINDOW, local_heads, HDIM
    )
    long_values = jnp.concatenate([previous[1], token_values]).reshape(
        local_rows + WINDOW, local_heads, HDIM
    )
    offset = lax.axis_index("tok") * local_rows
    block_rows = min(512, local_rows)
    query_place = offset + 0 + jnp.arange(block_rows, dtype=jnp.int32)
    key_place = offset + 0 - WINDOW + jnp.arange(block_rows + WINDOW, dtype=jnp.int32)
    pieces = attend_block(query_three, long_keys, long_values, query_place, key_place)
    return (pieces + normed).reshape(local_rows, local_heads * HDIM).astype(jnp.bfloat16)


def solution(mesh):
    placed = (
        P("tok", "head"),
        P("head", None),
        P("tok", "head"),
        P("tok", "head"),
        P("tok", "head"),
        P("head", None, None),
        P("head", None, None),
        P("head", None, None),
        P("head"),
        P("head"),
    )
    return jax.shard_map(
        on_device, mesh=mesh, in_specs=placed, out_specs=P("tok", "head"), check_vma=False
    )
```

profile of v0, /device:TPU:1, one launch (start us, length us, event | category | flops | bytes accessed | tf_op | source)
XLA Modules:
  0.0 233.7 jit_solution(14368238584306273980)
XLA Ops:
  6.5 1.5 copy.96
  8.1 3.8 %fusion.69 = f32[3,512,512]{1,2,0:T(8,128)} fusion(bf16[512,3,256]{0,2,1:T(8,128)(2,1)S(1)} %bitcast.162, f32[3,256,512]{2,1,0:T(8,128)} %param.15), kind=kOutput, calls=%fused_computation.94 | convolution fusion | flops 403046400 | bytes 5505024 | tf_op jit(solution)/shard_map/thd,hdf->thf/dot_general | solution.py:28
  11.9 2.3 fusion.71
  14.2 1.4 copy.97
  16.1 15.4 %all-reduce = f32[512,12]{0,1:T(8,128)S(1)} all-reduce(f32[512,12]{0,1:T(8,128)S(1)} %fusion.100), channel_id=2, replica_groups=mesh['tok'=32,'head'=4] {'head'}, use_global_device_ids=true, to_apply=%region_2.3.clone | all-reduce | flops 6144 | bytes 49152
  32.8 2.3 fusion.73
  35.2 3.3 %fusion.37 = f32[3,256,512]{1,2,0:T(8,128)S(1)} fusion(f32[3,512,512]{1,2,0:T(8,128)} %fusion.71, bf16[512,3,256]{0,2,1:T(8,128)(2,1)S(1)} %bitcast.171, f32[512,3]{0,1:T(4,128)S(1)} %compare_select_fusion, f32[3,512,512]{1,2,0:T(8,128)S(1)} %copy-done.10), kind=kOutput, calls=%fused_computation.71 | convolution fusion | flops 408944640 | bytes 8656896 | tf_op jit(solution)/shard_map/the,thf->hef/dot_general | solution.py:45
  38.5 1.7 fusion.43
  40.2 1.3 fusion.40
  41.5 2.5 %pad_maximum_fusion = f32[9,256,512]{1,2,0:T(8,128)} fusion(f32[3,256,512]{1,2,0:T(8,128)S(1)} %fusion.37, f32[3,256,512]{1,2,0:T(8,128)S(1)} %fusion.40, f32[3,256,512]{1,2,0:T(8,128)S(1)} %fusion.43), kind=kLoop, calls=%fused_computation.1 | loop fusion | flops 2359296 | bytes 9437184 | tf_op jit(solution)/shard_map/concatenate | solution.py:46
  45.1 7.6 %collective-permute-start = (bf16[2,256,768]{1,2,0:T(8,128)(2,1)}, bf16[2,256,768]{1,2,0:T(8,128)(2,1)}, u32[]{:S(2)}, u32[]{:S(2)}) collective-permute-start(bf16[2,256,768]{1,2,0:T(8,128)(2,1)} %pad_maximum_fusion.1), channel_id=1, source_target_pairs={{0,4},{4,8},{8,12},{12,16},{16,20},{20,24},{24,28},{28,32},{32,36}... | collective-permute-start | bytes 2359304 | tf_op jit(solution)/shard_map/ppermute | solution.py:21
  52.7 3.0 %copy.137 = f32[3,256,512]{1,2,0:T(8,128)} copy(f32[3,256,512]{2,1,0:T(8,128)} %param.15) | data formatting | bytes 3145728 | tf_op args[5]
  55.7 3.1 %copy.140 = f32[3,256,512]{1,2,0:T(8,128)} copy(f32[3,256,512]{2,1,0:T(8,128)} %param.16) | data formatting | bytes 3145728 | tf_op args[6]
  59.2 1.4 copy.102
  61.1 3.8 %collective-permute-done = bf16[2,256,768]{1,2,0:T(8,128)(2,1)} collective-permute-done((bf16[2,256,768]{1,2,0:T(8,128)(2,1)}, bf16[2,256,768]{1,2,0:T(8,128)(2,1)}, u32[]{:S(2)}, u32[]{:S(2)}) %collective-permute-start) | collective-permute-done | bytes 786464 | tf_op jit(solution)/shard_map/ppermute | solution.py:21
  64.9 1.2 fusion.96
  67.1 4.5 %fusion.97 = (f32[3,512]{1,0:T(4,128)S(1)}, f32[3,512,768]{1,2,0:T(8,128)}) fusion(f32[3,768,512]{2,1,0:T(8,128)S(1)} %fusion.50, pred[512,768]{0,1:T(8,128)(4,1)S(1)} %and_and_fusion), kind=kOutput, calls=%fused_computation.130 | output fusion | flops 7078655 | bytes 9836544 | tf_op jit(solution)/shard_map/sub | solution.py:70
  71.6 90.6 %all-reduce.3.cloned.1.call-done = f32[9,256,512]{1,2,0:T(8,128)} async-done(((f32[9,256,512]{1,2,0:T(8,128)}), f32[9,256,512]{1,2,0:T(8,128)}) %all-reduce.3.cloned.1.call-update) | async-done | bytes 4718608 | tf_op jit(solution)/shard_map/psum | solution.py:103
  162.1 3.0 %multiply_reduce_fusion = f32[9]{0:T(128)S(1)} fusion(f32[9,256,512]{1,2,0:T(8,128)} %all-reduce.3.cloned.1.call-done), kind=kLoop, calls=%fused_computation.9 | loop fusion | flops 2359287 | bytes 4718628 | tf_op jit(solution)/shard_map/reduce_sum | solution.py:104
  166.4 1.9 convolution_convert_fusion.4
  168.3 4.8 %add_convert_fusion.4 = bf16[9,256,512]{1,2,0:T(8,128)(2,1)} fusion(bf16[9,256,512]{1,2,0:T(8,128)(2,1)S(1)} %divide_convert_fusion, bf16[9,256,256]{2,1,0:T(8,128)(2,1)} %convolution_convert_fusion.4), kind=kOutput, calls=%fused_computation.7 | convolution fusion | flops 913637376 | bytes 5898240 | tf_op jit(solution)/shard_map/mij,mjk->mik/dot_general | solution.py:55
  173.1 4.4 %convolution_convert_fusion.3 = bf16[9,256,256]{2,1,0:T(8,128)(2,1)} fusion(bf16[9,256,512]{1,2,0:T(8,128)(2,1)} %add_convert_fusion.4), kind=kOutput, calls=%fused_computation.69 | convolution fusion | flops 604569600 | bytes 3538944 | tf_op jit(solution)/shard_map/mik,mjk->mij/dot_general | solution.py:50
  177.5 4.8 %add_convert_fusion.3 = bf16[9,256,512]{1,2,0:T(8,128)(2,1)} fusion(bf16[9,256,512]{1,2,0:T(8,128)(2,1)S(1)} %copy-done.3, bf16[9,256,256]{2,1,0:T(8,128)(2,1)} %convolution_convert_fusion.3), kind=kOutput, calls=%fused_computation.6 | convolution fusion | flops 913637376 | bytes 5898240 | tf_op jit(solution)/shard_map/mij,mjk->mik/dot_general | solution.py:55
  182.3 4.4 %convolution_convert_fusion.2 = bf16[9,256,256]{2,1,0:T(8,128)(2,1)} fusion(bf16[9,256,512]{1,2,0:T(8,128)(2,1)} %add_convert_fusion.3), kind=kOutput, calls=%fused_computation.68 | convolution fusion | flops 604569600 | bytes 3538944 | tf_op jit(solution)/shard_map/mik,mjk->mij/dot_general | solution.py:50
  186.7 4.8 %add_convert_fusion.2 = bf16[9,256,512]{1,2,0:T(8,128)(2,1)} fusion(bf16[9,256,512]{1,2,0:T(8,128)(2,1)S(1)} %copy-done.4, bf16[9,256,256]{2,1,0:T(8,128)(2,1)} %convolution_convert_fusion.2), kind=kOutput, calls=%fused_computation.5 | convolution fusion | flops 913637376 | bytes 5898240 | tf_op jit(solution)/shard_map/mij,mjk->mik/dot_general | solution.py:55
  191.6 4.6 %convolution_convert_fusion.1 = bf16[9,256,256]{2,1,0:T(8,128)(2,1)} fusion(bf16[9,256,512]{1,2,0:T(8,128)(2,1)} %add_convert_fusion.2), kind=kOutput, calls=%fused_computation.67 | convolution fusion | flops 604569600 | bytes 3538944 | tf_op jit(solution)/shard_map/mik,mjk->mij/dot_general | solution.py:50
  196.2 4.8 %add_convert_fusion.1 = bf16[9,256,512]{1,2,0:T(8,128)(2,1)} fusion(bf16[9,256,512]{1,2,0:T(8,128)(2,1)S(1)} %copy-done.5, bf16[9,256,256]{2,1,0:T(8,128)(2,1)} %convolution_convert_fusion.1), kind=kOutput, calls=%fused_computation.4 | convolution fusion | flops 913637376 | bytes 5898240 | tf_op jit(solution)/shard_map/mij,mjk->mik/dot_general | solution.py:55
  201.0 4.4 %convolution_convert_fusion = bf16[9,256,256]{2,1,0:T(8,128)(2,1)} fusion(bf16[9,256,512]{1,2,0:T(8,128)(2,1)} %add_convert_fusion.1), kind=kOutput, calls=%fused_computation.66 | convolution fusion | flops 604569600 | bytes 3538944 | tf_op jit(solution)/shard_map/mik,mjk->mij/dot_general | solution.py:50
  205.4 5.6 %fusion.15 = f32[9,256,512]{1,2,0:T(8,128)} fusion(bf16[9,256,512]{1,2,0:T(8,128)(2,1)S(1)} %copy-done.6, bf16[9,256,256]{2,1,0:T(8,128)(2,1)} %convolution_convert_fusion), kind=kOutput, calls=%fused_computation.35 | convolution fusion | flops 914817024 | bytes 8257536 | tf_op jit(solution)/shard_map/mij,mjk->mik/dot_general | solution.py:55
  211.0 4.2 %fusion.65 = f32[3,512,512]{1,2,0:T(8,128)} fusion(bf16[512,3,256]{0,2,1:T(8,128)(2,1)S(1)} %bitcast.168, f32[3,256,512]{1,2,0:T(8,128)} %copy.137, f32[9,256,512]{1,2,0:T(8,128)} %fusion.15, f32[3]{0:T(128)S(1)} %copy-done.14), kind=kOutput, calls=%fused_computation.92 | convolution fusion | flops 403832832 | bytes 7077900 | tf_op jit(solution)/shard_map/thd,hdf->thf/dot_general | solution.py:117
  215.2 6.7 %fusion.31 = (f32[512,3]{0,1:T(4,128)S(1)}, f32[3,256,512]{2,1,0:T(8,128)}) fusion(f32[3,512,512]{1,2,0:T(8,128)} %fusion.65, bf16[512,3,256]{0,2,1:T(8,128)(2,1)S(1)} %bitcast.169, f32[3,256,512]{1,2,0:T(8,128)} %copy.140, f32[9,256,512]{1,2,0:T(8,128)} %fusion.15, f32[3]{0:T(128)S(1)} %copy-done.14, f32[3,512,256]{2,1,0:T(8,128)} %param.17), kind=kOutput, calls=%fused_computation.59 | convolution fusion | flops 813169152 | bytes 11803648 | tf_op jit(solution)/shard_map/thf,hfe->the/dot_general | solution.py:122
  221.9 3.8 %fusion.34 = bf16[512,3,256]{0,2,1:T(8,128)(2,1)S(1)} fusion(f32[3,256,512]{2,1,0:T(8,128)} %get-tuple-element.10, f32[3,512,768]{1,2,0:T(8,128)} %get-tuple-element.8, f32[3,512]{1,0:T(4,128)S(1)} %get-tuple-element.7, bf16[512,3,256]{0,2,1:T(8,128)(2,1)S(1)} %bitcast.172, bf16[256,3,256]{0,2,1:T(8,128)(2,1)S(1)} %bitcast.175, f32[3,256]{1,0:T(4,128)S(1)} %mul.178, ...), kind=kOutput, calls=%fused_computation.62 | convolution fusion | flops 610271232 | bytes 8272896 | tf_op jit(solution)/shard_map/hqk,khd->qhd/dot_general | solution.py:72
  (51 shorter events, 6.3 us)
Async XLA Ops:
  6.5 9.1 %copy-start = (bf16[512,1280]{1,0:T(8,128)(2,1)S(1)}, bf16[512,1280]{1,0:T(8,128)(2,1)}, u32[]{:S(2)}) copy-start(bf16[512,1280]{1,0:T(8,128)(2,1)} %param.10) | copy-start | bytes 3932164
  6.5 155.6 %all-reduce.3.cloned.1.call-start = ((), (), s32[]{:S(2)}) async-start(), calls=%async_computation | async-start | bytes 9437184 | tf_op jit(solution)/shard_map/psum | solution.py:103
  8.1 3.8 %copy-start.7 = (f32[3,256,512]{2,1,0:T(8,128)S(1)}, f32[3,256,512]{2,1,0:T(8,128)}, u32[]{:S(2)}) copy-start(f32[3,256,512]{2,1,0:T(8,128)} %param.16) | copy-start | bytes 4718596
  11.9 3.7 %copy-start.12 = (bf16[1280,12]{0,1:T(8,128)(2,1)S(1)}, bf16[1280,12]{0,1:T(8,128)(2,1)}, u32[]{:S(2)}) copy-start(bf16[1280,12]{0,1:T(8,128)(2,1)} %param.11) | copy-start | bytes 92164
  14.2 17.3 %copy-start.15 = (u32[128]{0:T(128)S(1)}, u32[128]{0:T(128)}, u32[]{:S(2)}) copy-start(u32[128]{0:T(128)} %constant.46) | copy-start | bytes 1540
  15.6 28.5 %copy-start.8 = (bf16[512,768]{0,1:T(8,128)(2,1)}, bf16[512,768]{0,1:T(8,128)(2,1)S(1)}, u32[]{:S(2)}) copy-start(bf16[512,768]{0,1:T(8,128)(2,1)S(1)} %copy.97) | copy-start | bytes 2359300
  32.8 2.4 %copy-start.10 = (f32[3,512,512]{1,2,0:T(8,128)S(1)}, f32[3,512,512]{1,2,0:T(8,128)}, u32[]{:S(2)}) copy-start(f32[3,512,512]{1,2,0:T(8,128)} %fusion.69) | copy-start | bytes 9437188
  35.2 3.4 %copy-start.11 = (f32[3,512,512]{1,2,0:T(8,128)S(1)}, f32[3,512,512]{1,2,0:T(8,128)}, u32[]{:S(2)}) copy-start(f32[3,512,512]{1,2,0:T(8,128)} %fusion.71) | copy-start | bytes 9437188
  45.1 19.8 %collective-permute-start = (bf16[2,256,768]{1,2,0:T(8,128)(2,1)}, bf16[2,256,768]{1,2,0:T(8,128)(2,1)}, u32[]{:S(2)}, u32[]{:S(2)}) collective-permute-start(bf16[2,256,768]{1,2,0:T(8,128)(2,1)} %pad_maximum_fusion.1), channel_id=1, source_target_pairs={{0,4},{4,8},{8,12},{12,16},{16,20},{20,24},{24,28},{28,32},{32,36}... | collective-permute-start | bytes 2359304 | tf_op jit(solution)/shard_map/ppermute | solution.py:21
  58.9 1.7 copy-start.13
  162.1 3.8 %copy-start.2 = (f32[9,256,512]{1,2,0:T(8,128)S(1)}, f32[9,256,512]{1,2,0:T(8,128)}, u32[]{:S(2)}) copy-start(f32[9,256,512]{1,2,0:T(8,128)} %all-reduce.3.cloned.1.call-done) | copy-start | bytes 14155780
  173.1 4.4 %copy-start.3 = (bf16[9,256,512]{1,2,0:T(8,128)(2,1)S(1)}, bf16[9,256,512]{1,2,0:T(8,128)(2,1)}, u32[]{:S(2)}) copy-start(bf16[9,256,512]{1,2,0:T(8,128)(2,1)} %add_convert_fusion.4) | copy-start | bytes 7077892
  182.3 4.4 %copy-start.4 = (bf16[9,256,512]{1,2,0:T(8,128)(2,1)S(1)}, bf16[9,256,512]{1,2,0:T(8,128)(2,1)}, u32[]{:S(2)}) copy-start(bf16[9,256,512]{1,2,0:T(8,128)(2,1)} %add_convert_fusion.3) | copy-start | bytes 7077892
  191.6 4.6 %copy-start.5 = (bf16[9,256,512]{1,2,0:T(8,128)(2,1)S(1)}, bf16[9,256,512]{1,2,0:T(8,128)(2,1)}, u32[]{:S(2)}) copy-start(bf16[9,256,512]{1,2,0:T(8,128)(2,1)} %add_convert_fusion.2) | copy-start | bytes 7077892
  201.0 4.4 %copy-start.6 = (bf16[9,256,512]{1,2,0:T(8,128)(2,1)S(1)}, bf16[9,256,512]{1,2,0:T(8,128)(2,1)}, u32[]{:S(2)}) copy-start(bf16[9,256,512]{1,2,0:T(8,128)(2,1)} %add_convert_fusion.1) | copy-start | bytes 7077892
  205.4 5.6 %copy-start.14 = (f32[3]{0:T(128)S(1)}, f32[3]{0:T(128)}, u32[]{:S(2)}) copy-start(f32[3]{0:T(128)} %param.18) | copy-start | bytes 40
  215.2 6.7 %copy-start.9 = (bf16[512,768]{0,1:T(8,128)(2,1)S(1)}, bf16[512,768]{0,1:T(8,128)(2,1)}, u32[]{:S(2)}) copy-start(bf16[512,768]{0,1:T(8,128)(2,1)} %copy-done.8) | copy-start | bytes 2359300
  221.9 4.9 %copy-start.1 = (bf16[512,1280]{1,0:T(8,128)(2,1)S(1)}, bf16[512,1280]{1,0:T(8,128)(2,1)}, u32[]{:S(2)}) copy-start(bf16[512,1280]{1,0:T(8,128)(2,1)} %param.10) | copy-start | bytes 3932164
Sparse Core Ops, SparseCore 0:
  44.2 117.8 all-reduce.2
where the time goes:
time: 234 us
  waiting for transfers between devices  94.4 us (40%)
  matrix products  75.2 us (32%)
  blocking collectives  15.4 us (7%)
  local copies, waits for them, and re-layouts  14.9 us (6%)
  between operations  14.3 us (6%)
  other arithmetic  11.9 us (5%)
  starting transfers between devices  7.61 us (3%)
    psum x1, waiting for transfers between devices, on_device(): summed = lax.psum(stacked, 'tok')  90.6 us
    dot_general x5, matrix products, polish(): jnp.einsum('mij,mjk->mik', mixing, iterate, preferred_element_type=jnp.fl...  24.8 us
    dot_general x5, matrix products, polish(): jnp.einsum('mik,mjk->mij', iterate, iterate, preferred_element_type=jnp.f...  19.8 us
    unnamed x1, blocking collectives  15.4 us
    unnamed x38, local copies, waits for them, and re-layouts  12 us
    ppermute x1, starting transfers between devices, passed_along(): return lax.ppermute(block, axis, route)  7.61 us
    dot_general x1, matrix products, on_device(): jnp.einsum('thf,hfe->the', fast_hidden, new_second, preferred_element_typ...  6.68 us
  transfers between devices with their start and end apart: 2, of which 2 were waited for; matrix products, arithmetic and copies ran while one was open for 7% of the time, Pallas kernels for 0%

commit v1 on v0

v1 whole, which is shorter than its diff:
```python
import functools

import jax
import jax.numpy as jnp
from jax import lax
from jax.experimental import pallas as pl
from jax.experimental.pallas import tpu as pltpu
from jax.sharding import PartitionSpec as P

MESH = pl.DeviceIdType.MESH
HDIM = 256
FFN = 512
HALF = 128
ROWS = 512
HEADS = 3
MATS = 9
STEPS = 5
COEF_A = 3.4445
COEF_B = -4.775
COEF_C = 2.0315
EPS_SCALE = 1e-07
EPS_RMS = 1e-06
F32 = jnp.float32
BF16 = jnp.bfloat16

PLACE = [(m % 2, m // 2, m % 2) for m in range(8)] + [(0, 0, 2)]


def dot(a, b):
    return jnp.dot(a, b, preferred_element_type=F32)


def dot_nt(a, b):
    return lax.dot_general(a, b, (((1,), (1,)), ((), ())), preferred_element_type=F32)


def kernel(
    x_hbm, rw_hbm, q_hbm, k_hbm, v_hbm, w1_hbm, w3_hbm, w2_hbm, scale_ref, gain_ref, out_ref,
    xin, rw, q, k, v, w1, w3, w2, load_sem,
    lpad, lg, lrx, lss, lrs,
    hk, hv, hss, hrs,
    pg, pu, hd, kt, vt, att,
    gown, gs0, rx0, gs1, rx1, gs2, rx2, gfull, oall,
    ss0, rs0, ss1, rs1, ss2, rs2, ssx, rsx, ss3, rs3, ss4, rs4,
):
    tok = lax.axis_index("tok")
    z = lax.axis_index("head")
    c = lax.rem(tok, 2)
    x = lax.rem(lax.div(tok, 2), 4)
    y = lax.div(tok, 8)
    where = (x, y)

    def on_axis(axis, place):
        if axis == 0:
            return ((y * 4 + place) * 2 + c, z)
        return ((place * 4 + x) * 2 + c, z)

    sibling = (tok + 1 - 2 * c, z)

    def remote(src, dst, send, recv, device):
        return pltpu.make_async_remote_copy(
            src_ref=src, dst_ref=dst, send_sem=send, recv_sem=recv, device_id=device, device_id_type=MESH
        )

    loads = [
        pltpu.make_async_copy(a, b, load_sem.at[i])
        for i, (a, b) in enumerate(
            [(x_hbm, xin), (rw_hbm, rw), (k_hbm, k), (v_hbm, v), (w1_hbm, w1), (w3_hbm, w3), (w2_hbm, w2), (q_hbm, q)]
        )
    ]
    for load in loads:
        load.start()

    barrier = pltpu.get_barrier_semaphore()

    def greet(device):
        pl.semaphore_signal(barrier, inc=1, device_id=device, device_id_type=MESH)

    greet(sibling)
    for d in range(1, 4):
        greet(on_axis(0, lax.rem(x + d, 4)))
        greet(on_axis(1, lax.rem(y + d, 4)))
        greet((tok, lax.rem(z + d, 4)))

    greet((lax.rem(tok + 31, 32), z))
    greet((lax.rem(tok + 1, 32), z))

    lpad[...] = jnp.zeros_like(lpad)
    lg[...] = jnp.zeros_like(lg)
    gfull[2] = jnp.zeros((HDIM, FFN), BF16)
    loads[0].wait()
    loads[1].wait()
    lpad[:, 0:12] = dot(xin[...], rw[...])
    turned = lpad[...].T
    for head in range(4):
        lg[head, 0:HEADS, :] = turned[HEADS * head : HEADS * (head + 1)]
    loads[2].wait()
    loads[3].wait()

    pl.semaphore_wait(barrier, 12)

    logit_copies = []
    for d in range(1, 4):
        there = lax.rem(z + d, 4)
        copy = remote(lg.at[there], lrx.at[d - 1], lss.at[d - 1], lrs.at[d - 1], (tok, there))
        copy.start()
        logit_copies.append(copy)

    halo = [
        remote(k.at[pl.ds(ROWS - HDIM, HDIM)], hk, hss.at[0], hrs.at[0], (tok + 1, z)),
        remote(v.at[pl.ds(ROWS - HDIM, HDIM)], hv, hss.at[1], hrs.at[1], (tok + 1, z)),
    ]

    @pl.when(tok < 31)
    def _():
        for copy in halo:
            copy.start()

    @pl.when(tok == 0)
    def _():
        hk[...] = jnp.zeros_like(hk)
        hv[...] = jnp.zeros_like(hv)

    for load in loads[4:7]:
        load.wait()

    def before_rates(h, carry):
        columns = pl.ds(pl.multiple_of(h * HDIM, HDIM), HDIM)
        first = w1[h].astype(BF16)
        third = w3[h].astype(BF16)
        second = w2[h].astype(BF16)
        for part in range(2):
            rows = pl.ds(part * HDIM, HDIM)
            keys = k[rows, columns]
            values = v[rows, columns]
            kt[h, :, rows] = keys.T
            vt[h, :, rows] = values.T
            gate = dot(keys, first)
            up = dot(keys, third)
            back = -dot_nt(values, second)
            sig = jax.nn.sigmoid(gate)
            activ = gate * sig
            pg[h, rows, :] = back * up * sig * (1.0 + gate * (1.0 - sig))
            pu[h, rows, :] = back * activ
            hd[h, rows, :] = -(activ * up)
        return carry

    lax.fori_loop(0, HEADS, before_rates, 0)

    for copy in logit_copies:
        copy.wait_recv()
    logits = lg[z] + lrx[0] + lrx[1] + lrx[2]
    rates = jnp.maximum(logits, 0.0) + jnp.log1p(jnp.exp(-jnp.abs(logits)))
    rates_down = rates.T

    mine = pl.ds(pl.multiple_of(c * HALF, HALF), HALF)
    other = pl.ds(pl.multiple_of(HALF - c * HALF, HALF), HALF)

    s0 = [
        remote(gs0.at[m], rx0.at[m], ss0.at[m], rs0.at[m], sibling) for m in range(MATS)
    ]
    s1 = []
    for m in range(MATS):
        axis, place, slot = PLACE[m]
        step = lax.rem(place - where[axis] + 4, 4)
        index = jnp.maximum(step - 1, 0)
        s1.append(
            remote(gs1.at[m], rx1.at[slot, index], ss1.at[m], rs1.at[slot, index], on_axis(axis, place))
        )

    def send_chip_sum(m):
        axis, place, slot = PLACE[m]
        s0[m].wait_recv()
        both = gown[m] + rx0[m].astype(F32)
        gown[m] = both
        gs1[m] = both.astype(BF16)

        @pl.when(where[axis] != place)
        def _():
            s1[m].start()

    for h in range(HEADS):
        rate = rates_down[:, h : h + 1]
        wides = ((kt, pg), (kt, pu), (vt, hd))
        for j, (left, right) in enumerate(wides):
            m = 3 * h + j
            scaled = (rate * right[h]).astype(BF16)
            gs0[m] = dot(left[h, other, :], scaled).astype(BF16)
            s0[m].start()
            gown[m] = dot(left[h, mine, :], scaled)
            if m > 1:
                send_chip_sum(m - 2)
    send_chip_sum(MATS - 2)
    send_chip_sum(MATS - 1)

    loads[7].wait()

    @pl.when(tok > 0)
    def _():
        for copy in halo:
            copy.wait_recv()

    row = lax.broadcasted_iota(jnp.int32, (HDIM, HDIM), 0)
    column = lax.broadcasted_iota(jnp.int32, (HDIM, HDIM), 1)
    has_past = tok > 0

    def attend(h, carry):
        columns = pl.ds(pl.multiple_of(h * HDIM, HDIM), HDIM)
        low, high = pl.ds(0, HDIM), pl.ds(HDIM, HDIM)
        blocks = (
            (low, hk[:, columns], hv[:, columns], k[low, columns], v[low, columns], True),
            (high, k[low, columns], v[low, columns], k[high, columns], v[high, columns], False),
        )
        for rows, old_k, old_v, new_k, new_v, edge in blocks:
            queries = q[rows, columns]
            seen = column > row
            if edge:
                seen = jnp.logical_and(seen, has_past)
            old = jnp.where(seen, dot_nt(queries, old_k) * HDIM ** (-0.5), -1e30)
            new = jnp.where(column <= row, dot_nt(queries, new_k) * HDIM ** (-0.5), -1e30)
            top = jnp.maximum(jnp.max(old, axis=1, keepdims=True), jnp.max(new, axis=1, keepdims=True))
            old = jnp.exp(old - top)
            new = jnp.exp(new - top)
            total = jnp.sum(old, axis=1, keepdims=True) + jnp.sum(new, axis=1, keepdims=True)
            mixed = dot(old.astype(BF16), old_v) + dot(new.astype(BF16), new_v)
            att[rows, columns] = mixed / total
        return carry

    lax.fori_loop(0, HEADS, attend, 0)

    owned = (2 * x, 2 * y + 1, 8)
    second_copies = []
    for slot in range(3):
        axis = (0, 1, 0)[slot]
        second_copies.append(
            [
                remote(
                    gs2.at[slot], rx2.at[slot, d - 1], ss2.at[slot, d - 1], rs2.at[slot, d - 1],
                    on_axis(1 - axis, lax.rem(where[1 - axis] + d, 4)),
                )
                for d in range(1, 4)
            ]
        )
    third_copies = [
        [
            remote(
                oall.at[owned[slot], mine], oall.at[owned[slot], mine], ss3.at[slot, d - 1], rs3.at[owned[slot]],
                on_axis((0, 1, 0)[slot], lax.rem(where[(0, 1, 0)[slot]] + d, 4)),
            )
            for d in range(1, 4)
        ]
        for slot in range(3)
    ]
    half_copies = [
        remote(gfull.at[slot, mine], gfull.at[slot, mine], ssx.at[slot], rsx.at[slot], sibling) for slot in range(3)
    ]

    def if_there(slot, action):
        if slot < 2:
            action()
        else:
            pl.when(x == 0)(action)

    def arrived_first(slot):
        m = owned[slot]
        total = gown[m]
        for d in range(3):
            remote(gs1.at[m], rx1.at[slot, d], ss1.at[m], rs1.at[slot, d], sibling).wait_recv()
            total = total + rx1[slot, d].astype(F32)
        gown[m] = total
        gs2[slot] = total.astype(BF16)
        for copy in second_copies[slot]:
            copy.start()

    def arrived_second(slot):
        total = gown[owned[slot]]
        for d, copy in enumerate(second_copies[slot]):
            copy.wait_recv()
            total = total + rx2[slot, d].astype(F32)
        gfull[slot, mine, :] = total.astype(BF16)
        half_copies[slot].start()

    for slot in range(3):
        if_there(slot, functools.partial(arrived_first, slot))
    for slot in range(3):
        if_there(slot, functools.partial(arrived_second, slot))
    for slot in range(3):
        if_there(slot, half_copies[slot].wait_recv)

    iterates = []
    for slot in range(3):
        full = gfull[slot].astype(F32)
        norm = jnp.sqrt(jnp.sum(full * full, keepdims=True)) + EPS_SCALE
        iterates.append((full / norm).astype(BF16))
    for repeat in range(STEPS):
        grams = [dot_nt(it, it).astype(BF16) for it in iterates]
        mixing = [
            (COEF_B * gram.astype(F32) + COEF_C * dot(gram, gram)).astype(BF16) for gram in grams
        ]
        iterates = [
            (COEF_A * it.astype(F32) + dot(mix, it)).astype(BF16) for mix, it in zip(mixing, iterates)
        ]

    def publish(slot):
        oall[owned[slot]] = iterates[slot]
        for copy in third_copies[slot]:
            copy.start()

    for slot in range(3):
        if_there(slot, functools.partial(publish, slot))

    fourth_copies = [
        remote(oall.at[m, mine], oall.at[m, mine], ss4.at[m], rs4.at[m], sibling) for m in range(MATS)
    ]

    def foreign(m, action):
        axis, place, slot = PLACE[m]
        pl.when(where[axis] != place)(action)

    def forward(m):
        def action():
            remote(oall.at[m, mine], oall.at[m, mine], ss4.at[m], rs3.at[m], sibling).wait_recv()
            fourth_copies[m].start()

        foreign(m, action)

    def apply(h):
        for j in range(3):
            foreign(3 * h + j, fourth_copies[3 * h + j].wait_recv)
        columns = pl.ds(h * HDIM, HDIM)
        size = scale_ref[h]
        first = (w1[h] - size * oall[3 * h].astype(F32)).astype(BF16)
        third = (w3[h] - size * oall[3 * h + 1].astype(F32)).astype(BF16)
        second = (w2[h] - size * oall[3 * h + 2].astype(F32).T).astype(BF16)
        gain = gain_ref[:, h * HDIM : (h + 1) * HDIM]
        for part in range(2):
            rows = pl.ds(part * HDIM, HDIM)
            queries = q[rows, columns]
            gate = dot(queries, first)
            up = dot(queries, third)
            hidden = (gate * jax.nn.sigmoid(gate) * up).astype(BF16)
            fast = dot(hidden, second)
            spread = jnp.mean(fast * fast, axis=1, keepdims=True)
            normed = fast * lax.rsqrt(spread + EPS_RMS) * gain
            out_ref[rows, columns] = (att[rows, columns] + normed).astype(BF16)

    for m in range(MATS):
        forward(m)
    for h in range(HEADS):
        apply(h)

    for copy in logit_copies + s0:
        copy.wait_send()

    @pl.when(tok < 31)
    def _():
        for copy in halo:
            copy.wait_send()

    for m in range(MATS):
        foreign(m, s1[m].wait_send)
        foreign(m, fourth_copies[m].wait_send)
    for slot in range(3):

        def finish(slot=slot):
            for copy in second_copies[slot] + [half_copies[slot]] + third_copies[slot]:
                copy.wait_send()

        if_there(slot, finish)


def on_device(x, rw, q, k, v, w1, w3, w2, scale, gain):
    anywhere = pl.BlockSpec(memory_space=pl.ANY)
    dma = pltpu.SemaphoreType.DMA
    features = x.shape[1]
    wide = HEADS * HDIM
    return pl.pallas_call(
        kernel,
        name="layer",
        out_shape=jax.ShapeDtypeStruct((ROWS, wide), BF16),
        in_specs=[anywhere] * 8
        + [pl.BlockSpec(memory_space=pltpu.SMEM), pl.BlockSpec(memory_space=pltpu.VMEM)],
        out_specs=pl.BlockSpec(memory_space=pltpu.VMEM),
        scratch_shapes=[
            pltpu.VMEM((ROWS, features), BF16),
            pltpu.VMEM(rw.shape, BF16),
            pltpu.VMEM((ROWS, wide), BF16),
            pltpu.VMEM((ROWS, wide), BF16),
            pltpu.VMEM((ROWS, wide), BF16),
            pltpu.VMEM((HEADS, HDIM, FFN), F32),
            pltpu.VMEM((HEADS, HDIM, FFN), F32),
            pltpu.VMEM((HEADS, FFN, HDIM), F32),
            dma((8,)),
            pltpu.VMEM((ROWS, 128), F32),
            pltpu.VMEM((4, 8, ROWS), F32),
            pltpu.VMEM((3, 8, ROWS), F32),
            dma((3,)),
            dma((3,)),
            pltpu.VMEM((HDIM, wide), BF16),
            pltpu.VMEM((HDIM, wide), BF16),
            dma((2,)),
            dma((2,)),
            pltpu.VMEM((HEADS, ROWS, FFN), F32),
            pltpu.VMEM((HEADS, ROWS, FFN), F32),
            pltpu.VMEM((HEADS, ROWS, FFN), F32),
            pltpu.VMEM((HEADS, HDIM, ROWS), BF16),
            pltpu.VMEM((HEADS, HDIM, ROWS), BF16),
            pltpu.VMEM((ROWS, wide), F32),
            pltpu.VMEM((MATS, HALF, FFN), F32),
            pltpu.VMEM((MATS, HALF, FFN), BF16),
            pltpu.VMEM((MATS, HALF, FFN), BF16),
            pltpu.VMEM((MATS, HALF, FFN), BF16),
            pltpu.VMEM((3, 3, HALF, FFN), BF16),
            pltpu.VMEM((3, HALF, FFN), BF16),
            pltpu.VMEM((3, 3, HALF, FFN), BF16),
            pltpu.VMEM((3, HDIM, FFN), BF16),
            pltpu.VMEM((MATS, HDIM, FFN), BF16),
            dma((MATS,)),
            dma((MATS,)),
            dma((MATS,)),
            dma((3, 3)),
            dma((3, 3)),
            dma((3, 3)),
            dma((3,)),
            dma((3,)),
            dma((3, 3)),
            dma((MATS,)),
            dma((MATS,)),
            dma((MATS,)),
        ],
        compiler_params=pltpu.CompilerParams(
            collective_id=0, has_side_effects=True, vmem_limit_bytes=56 << 20
        ),
    )(x, rw, q, k, v, w1, w3, w2, scale, gain.reshape(1, wide))


def solution(mesh):
    placed = (
        P("tok", "head"),
        P("head", None),
        P("tok", "head"),
        P("tok", "head"),
        P("tok", "head"),
        P("head", None, None),
        P("head", None, None),
        P("head", None, None),
        P("head"),
        P("head"),
    )
    return jax.shard_map(
        on_device, mesh=mesh, in_specs=placed, out_specs=P("tok", "head"), check_vma=False
    )
```

time: 234 us -> 66.6 us (0.28)
  the two profiles are of different devices: /device:TPU:1 before, /device:TPU:101 now
where the time goes in v1:
time: 66.6 us; the launch traced here: 66.4 us
  Pallas kernels  61.3 us (92%)
  local copies, waits for them, and re-layouts  5.04 us (8%)
    pallas_call x1, Pallas kernels, on_device(): pl.pallas_call(kernel, name='layer', out_shape=jax.ShapeDtypeStruct((ROWS...  61.3 us
    unnamed x2, local copies, waits for them, and re-layouts  3.77 us

profile of v1, /device:TPU:101, one launch (start us, length us, event | category | flops | bytes accessed | tf_op | source)
XLA Modules:
  0.0 66.4 jit_solution(15992500499954384420)
XLA Ops:
  0.0 1.3 %reshape.3.gain_ref = f32[1,768]{1,0:T(1,128)} reshape(f32[768]{0:T(1024)} %param.19) | data formatting | bytes 6144 | tf_op jit(solution)/shard_map/reshape | solution.py:434
  1.3 1.7 %copy.11.rw_hbm = bf16[1280,12]{1,0:T(8,128)(2,1)} copy(bf16[1280,12]{0,1:T(8,128)(2,1)} %param.11) | data formatting | bytes 61440 | tf_op args[1]
  3.0 61.3 %layer.1 = bf16[512,768]{1,0:T(8,128)(2,1)} custom-call(bf16[512,1280]{1,0:T(8,128)(2,1)} %x_hbm.1, bf16[1280,12]{1,0:T(8,128)(2,1)} %copy.11.rw_hbm, bf16[512,768]{1,0:T(8,128)(2,1)} %q_hbm.1, bf16[512,768]{1,0:T(8,128)(2,1)} %k_hbm.1, bf16[512,768]{1,0:T(8,128)(2,1)} %v_hbm.1, f32[3,256,512]{2,1,0:T(8,128)} %w1_hbm.1, f32[3,256,512]{2,1,0:T(8,128)} %w3_hbm.1, ...), custom_call_target="tpu_custom_call" | custom-call | tf_op jit(solution)/shard_map/layer/pallas_call | solution.py:377
  64.3 2.1 %copy.13 = bf16[512,768]{1,0:T(8,128)(2,1)} copy(bf16[512,768]{1,0:T(8,128)(2,1)} %layer.1) | data formatting | bytes 1572864

commit v2 on v1

--- a/solution.py
+++ b/solution.py
@@ -1,5 +1,3 @@
-import functools
-
 import jax
 import jax.numpy as jnp
 from jax import lax
@@ -23,7 +21,8 @@
 F32 = jnp.float32
 BF16 = jnp.bfloat16
 
-PLACE = [(m % 2, m // 2, m % 2) for m in range(8)] + [(0, 0, 2)]
+PLACE = [None] + [((m - 1) % 2, (m - 1) // 2) for m in range(1, MATS)]
+QUARTER = HALF // 4
 
 
 def dot(a, b):
@@ -40,6 +39,7 @@
     lpad, lg, lrx, lss, lrs,
     hk, hv, hss, hrs,
     pg, pu, hd, kt, vt, att,
+    eq, es, erx, ess, ers,
     gown, gs0, rx0, gs1, rx1, gs2, rx2, gfull, oall,
     ss0, rs0, ss1, rs1, ss2, rs2, ssx, rsx, ss3, rs3, ss4, rs4,
 ):
@@ -87,10 +87,9 @@
 
     lpad[...] = jnp.zeros_like(lpad)
     lg[...] = jnp.zeros_like(lg)
-    gfull[2] = jnp.zeros((HDIM, FFN), BF16)
     loads[0].wait()
     loads[1].wait()
-    lpad[:, 0:12] = dot(xin[...], rw[...])
+    lpad[:, 0:12] = dot_nt(xin[...], rw[...])
     turned = lpad[...].T
     for head in range(4):
         lg[head, 0:HEADS, :] = turned[HEADS * head : HEADS * (head + 1)]
@@ -159,21 +158,42 @@
     s0 = [
         remote(gs0.at[m], rx0.at[m], ss0.at[m], rs0.at[m], sibling) for m in range(MATS)
     ]
-    s1 = []
-    for m in range(MATS):
-        axis, place, slot = PLACE[m]
+    s1 = [None]
+    for m in range(1, MATS):
+        axis, place = PLACE[m]
         step = lax.rem(place - where[axis] + 4, 4)
         index = jnp.maximum(step - 1, 0)
         s1.append(
-            remote(gs1.at[m], rx1.at[slot, index], ss1.at[m], rs1.at[slot, index], on_axis(axis, place))
+            remote(gs1.at[m], rx1.at[axis, index], ss1.at[m], rs1.at[axis, index], on_axis(axis, place))
+        )
+
+    def quarter(place):
+        return pl.ds(pl.multiple_of(place * QUARTER, QUARTER), QUARTER)
+
+    my_quarter = quarter(c * 4 + x)
+    every = [[], [], []]
+    for d in (2, 1, 3):
+        x_there, y_there = lax.rem(x + d, 4), lax.rem(y + d, 4)
+        every[0].append(
+            remote(gs1.at[0, quarter(x_there)], erx.at[0, d - 1], ess.at[0, d - 1], ers.at[0, d - 1], on_axis(0, x_there))
+        )
+        every[1].append(remote(es, erx.at[1, d - 1], ess.at[1, d - 1], ers.at[1, d - 1], on_axis(1, y_there)))
+        every[2].append(
+            remote(
+                gfull.at[2, my_quarter], gfull.at[2, my_quarter], ess.at[2, d - 1], ers.at[2, d - 1], on_axis(0, x_there)
+            )
         )
 
     def send_chip_sum(m):
-        axis, place, slot = PLACE[m]
         s0[m].wait_recv()
         both = gown[m] + rx0[m].astype(F32)
         gown[m] = both
         gs1[m] = both.astype(BF16)
+        if m == 0:
+            for copy in every[0]:
+                copy.start()
+            return
+        axis, place = PLACE[m]
 
         @pl.when(where[axis] != place)
         def _():
@@ -192,6 +212,14 @@
                 send_chip_sum(m - 2)
     send_chip_sum(MATS - 2)
     send_chip_sum(MATS - 1)
+
+    for copy in every[0]:
+        copy.wait_recv()
+    total = gown[0, quarter(x), :] + erx[0, 0].astype(F32) + erx[0, 1].astype(F32) + erx[0, 2].astype(F32)
+    eq[...] = total
+    es[...] = total.astype(BF16)
+    for copy in every[1]:
+        copy.start()
 
     loads[7].wait()
 
@@ -228,40 +256,39 @@
 
     lax.fori_loop(0, HEADS, attend, 0)
 
-    owned = (2 * x, 2 * y + 1, 8)
-    second_copies = []
-    for slot in range(3):
-        axis = (0, 1, 0)[slot]
-        second_copies.append(
-            [
-                remote(
-                    gs2.at[slot], rx2.at[slot, d - 1], ss2.at[slot, d - 1], rs2.at[slot, d - 1],
-                    on_axis(1 - axis, lax.rem(where[1 - axis] + d, 4)),
-                )
-                for d in range(1, 4)
-            ]
-        )
+    for copy in every[1]:
+        copy.wait_recv()
+    total = eq[...] + erx[1, 0].astype(F32) + erx[1, 1].astype(F32) + erx[1, 2].astype(F32)
+    gfull[2, my_quarter, :] = total.astype(BF16)
+    for copy in every[2]:
+        copy.start()
+
+    owned = (2 * x + 1, 2 * y + 2)
+    second_copies = [
+        [
+            remote(
+                gs2.at[slot], rx2.at[slot, d - 1], ss2.at[slot, d - 1], rs2.at[slot, d - 1],
+                on_axis(1 - slot, lax.rem(where[1 - slot] + d, 4)),
+            )
+            for d in (2, 1, 3)
+        ]
+        for slot in range(2)
+    ]
     third_copies = [
         [
             remote(
                 oall.at[owned[slot], mine], oall.at[owned[slot], mine], ss3.at[slot, d - 1], rs3.at[owned[slot]],
-                on_axis((0, 1, 0)[slot], lax.rem(where[(0, 1, 0)[slot]] + d, 4)),
+                on_axis(slot, lax.rem(where[slot] + d, 4)),
             )
-            for d in range(1, 4)
+            for d in (2, 1, 3)
         ]
-        for slot in range(3)
+        for slot in range(2)
     ]
     half_copies = [
         remote(gfull.at[slot, mine], gfull.at[slot, mine], ssx.at[slot], rsx.at[slot], sibling) for slot in range(3)
     ]
 
-    def if_there(slot, action):
-        if slot < 2:
-            action()
-        else:
-            pl.when(x == 0)(action)
-
-    def arrived_first(slot):
+    for slot in range(2):
         m = owned[slot]
         total = gown[m]
         for d in range(3):
@@ -272,20 +299,22 @@
         for copy in second_copies[slot]:
             copy.start()
 
-    def arrived_second(slot):
+    for d, x_there in ((d, lax.rem(x + 4 - d, 4)) for d in (2, 1, 3)):
+        theirs = quarter(c * 4 + x_there)
+        remote(gfull.at[2, theirs], gfull.at[2, theirs], ess.at[2, d - 1], ers.at[2, d - 1], sibling).wait_recv()
+    half_copies[2].start()
+
+    for slot in range(2):
         total = gown[owned[slot]]
-        for d, copy in enumerate(second_copies[slot]):
+        for copy in second_copies[slot]:
             copy.wait_recv()
+        for d in range(3):
             total = total + rx2[slot, d].astype(F32)
         gfull[slot, mine, :] = total.astype(BF16)
         half_copies[slot].start()
 
-    for slot in range(3):
-        if_there(slot, functools.partial(arrived_first, slot))
-    for slot in range(3):
-        if_there(slot, functools.partial(arrived_second, slot))
-    for slot in range(3):
-        if_there(slot, half_copies[slot].wait_recv)
+    for copy in half_copies:
+        copy.wait_recv()
 
     iterates = []
     for slot in range(3):
@@ -301,21 +330,21 @@
             (COEF_A * it.astype(F32) + dot(mix, it)).astype(BF16) for mix, it in zip(mixing, iterates)
         ]
 
-    def publish(slot):
+    for slot in range(2):
         oall[owned[slot]] = iterates[slot]
-        for copy in third_copies[slot]:
+    for pair in zip(*third_copies):
+        for copy in pair:
             copy.start()
-
-    for slot in range(3):
-        if_there(slot, functools.partial(publish, slot))
+    oall[0] = iterates[2]
 
     fourth_copies = [
         remote(oall.at[m, mine], oall.at[m, mine], ss4.at[m], rs4.at[m], sibling) for m in range(MATS)
     ]
 
     def foreign(m, action):
-        axis, place, slot = PLACE[m]
-        pl.when(where[axis] != place)(action)
+        if m > 0:
+            axis, place = PLACE[m]
+            pl.when(where[axis] != place)(action)
 
     def forward(m):
         def action():
@@ -332,7 +361,7 @@
         first = (w1[h] - size * oall[3 * h].astype(F32)).astype(BF16)
         third = (w3[h] - size * oall[3 * h + 1].astype(F32)).astype(BF16)
         second = (w2[h] - size * oall[3 * h + 2].astype(F32).T).astype(BF16)
-        gain = gain_ref[:, h * HDIM : (h + 1) * HDIM]
+        gain = gain_ref[pl.ds(h * HDIM, HDIM)].reshape(1, HDIM)
         for part in range(2):
             rows = pl.ds(part * HDIM, HDIM)
             queries = q[rows, columns]
@@ -344,7 +373,7 @@
             normed = fast * lax.rsqrt(spread + EPS_RMS) * gain
             out_ref[rows, columns] = (att[rows, columns] + normed).astype(BF16)
 
-    for m in range(MATS):
+    for m in range(1, MATS):
         forward(m)
     for h in range(HEADS):
         apply(h)
@@ -357,16 +386,12 @@
         for copy in halo:
             copy.wait_send()
 
-    for m in range(MATS):
+    for m in range(1, MATS):
         foreign(m, s1[m].wait_send)
         foreign(m, fourth_copies[m].wait_send)
-    for slot in range(3):
-
-        def finish(slot=slot):
-            for copy in second_copies[slot] + [half_copies[slot]] + third_copies[slot]:
-                copy.wait_send()
-
-        if_there(slot, finish)
+    for copies in every + second_copies + [half_copies] + third_copies:
+        for copy in copies:
+            copy.wait_send()
 
 
 def on_device(x, rw, q, k, v, w1, w3, w2, scale, gain):
@@ -383,7 +408,7 @@
         out_specs=pl.BlockSpec(memory_space=pltpu.VMEM),
         scratch_shapes=[
             pltpu.VMEM((ROWS, features), BF16),
-            pltpu.VMEM(rw.shape, BF16),
+            pltpu.VMEM((rw.shape[1], rw.shape[0]), BF16),
             pltpu.VMEM((ROWS, wide), BF16),
             pltpu.VMEM((ROWS, wide), BF16),
             pltpu.VMEM((ROWS, wide), BF16),
@@ -406,24 +431,29 @@
             pltpu.VMEM((HEADS, HDIM, ROWS), BF16),
             pltpu.VMEM((HEADS, HDIM, ROWS), BF16),
             pltpu.VMEM((ROWS, wide), F32),
+            pltpu.VMEM((QUARTER, FFN), F32),
+            pltpu.VMEM((QUARTER, FFN), BF16),
+            pltpu.VMEM((2, 3, QUARTER, FFN), BF16),
+            dma((3, 3)),
+            dma((3, 3)),
             pltpu.VMEM((MATS, HALF, FFN), F32),
             pltpu.VMEM((MATS, HALF, FFN), BF16),
             pltpu.VMEM((MATS, HALF, FFN), BF16),
             pltpu.VMEM((MATS, HALF, FFN), BF16),
-            pltpu.VMEM((3, 3, HALF, FFN), BF16),
-            pltpu.VMEM((3, HALF, FFN), BF16),
-            pltpu.VMEM((3, 3, HALF, FFN), BF16),
+            pltpu.VMEM((2, 3, HALF, FFN), BF16),
+            pltpu.VMEM((2, HALF, FFN), BF16),
+            pltpu.VMEM((2, 3, HALF, FFN), BF16),
             pltpu.VMEM((3, HDIM, FFN), BF16),
             pltpu.VMEM((MATS, HDIM, FFN), BF16),
             dma((MATS,)),
             dma((MATS,)),
             dma((MATS,)),
-            dma((3, 3)),
-            dma((3, 3)),
-            dma((3, 3)),
+            dma((2, 3)),
+            dma((2, 3)),
+            dma((2, 3)),
             dma((3,)),
             dma((3,)),
-            dma((3, 3)),
+            dma((2, 3)),
             dma((MATS,)),
             dma((MATS,)),
             dma((MATS,)),
@@ -431,7 +461,7 @@
         compiler_params=pltpu.CompilerParams(
             collective_id=0, has_side_effects=True, vmem_limit_bytes=56 << 20
         ),
-    )(x, rw, q, k, v, w1, w3, w2, scale, gain.reshape(1, wide))
+    )(x, rw.T, q, k, v, w1, w3, w2, scale, gain)
 
 
 def solution(mesh):

time: 66.6 us -> 55.6 us (0.83)
  the two profiles are of different devices: /device:TPU:101 before, /device:TPU:1 now
where the time goes in v2:
time: 55.6 us; the launch traced here: 55.4 us
  Pallas kernels  53.3 us (96%)
  local copies, waits for them, and re-layouts  2.06 us (4%)
    pallas_call x1, Pallas kernels, on_device(): pl.pallas_call(kernel, name='layer', out_shape=jax.ShapeDtypeStruct((ROWS...  53.3 us
    unnamed x1, local copies, waits for them, and re-layouts  2.06 us

profile of v2, /device:TPU:1, one launch (start us, length us, event | category | flops | bytes accessed | tf_op | source)
XLA Modules:
  0.0 55.4 jit_solution(3478285388831236512)
XLA Ops:
  0.0 53.3 %layer.1 = bf16[512,768]{1,0:T(8,128)(2,1)} custom-call(bf16[512,1280]{1,0:T(8,128)(2,1)} %x_hbm.1, bf16[12,1280]{1,0:T(8,128)(2,1)} %bitcast.1, bf16[512,768]{1,0:T(8,128)(2,1)} %q_hbm.1, bf16[512,768]{1,0:T(8,128)(2,1)} %k_hbm.1, bf16[512,768]{1,0:T(8,128)(2,1)} %v_hbm.1, f32[3,256,512]{2,1,0:T(8,128)} %w1_hbm.1, f32[3,256,512]{2,1,0:T(8,128)} %w3_hbm.1, ...), custom_call_target="tpu_custom_call" | custom-call | tf_op jit(solution)/shard_map/layer/pallas_call | solution.py:402
  53.4 2.1 %copy.12 = bf16[512,768]{1,0:T(8,128)(2,1)} copy(bf16[512,768]{1,0:T(8,128)(2,1)} %layer.1) | data formatting | bytes 1572864

commit v3 on v2

--- a/solution.py
+++ b/solution.py
@@ -23,6 +23,7 @@
 
 PLACE = [None] + [((m - 1) % 2, (m - 1) // 2) for m in range(1, MATS)]
 QUARTER = HALF // 4
+LAG = 5
 
 
 def dot(a, b):
@@ -38,7 +39,7 @@
     xin, rw, q, k, v, w1, w3, w2, load_sem,
     lpad, lg, lrx, lss, lrs,
     hk, hv, hss, hrs,
-    pg, pu, hd, kt, vt, att,
+    pg, pu, hd, kt, vt, att, whole,
     eq, es, erx, ess, ers,
     gown, gs0, rx0, gs1, rx1, gs2, rx2, gfull, oall,
     ss0, rs0, ss1, rs1, ss2, rs2, ssx, rsx, ss3, rs3, ss4, rs4,
@@ -62,14 +63,19 @@
             src_ref=src, dst_ref=dst, send_sem=send, recv_sem=recv, device_id=device, device_id_type=MESH
         )
 
-    loads = [
-        pltpu.make_async_copy(a, b, load_sem.at[i])
-        for i, (a, b) in enumerate(
-            [(x_hbm, xin), (rw_hbm, rw), (k_hbm, k), (v_hbm, v), (w1_hbm, w1), (w3_hbm, w3), (w2_hbm, w2), (q_hbm, q)]
-        )
-    ]
-    for load in loads:
-        load.start()
+    def load(source, target, number):
+        copy = pltpu.make_async_copy(source, target, load_sem.at[number])
+        copy.start()
+        return copy
+
+    load_x = load(x_hbm, xin, 0)
+    load_rw = load(rw_hbm, rw, 1)
+    load_kv = [load(k_hbm, k, 2), load(v_hbm, v, 3)]
+    load_w = [
+        [load(a.at[h], b.at[h], 4 + 3 * h + i) for i, (a, b) in enumerate(((w1_hbm, w1), (w3_hbm, w3), (w2_hbm, w2)))]
+        for h in range(HEADS)
+    ]
+    load_q = load(q_hbm, q, 13)
 
     barrier = pltpu.get_barrier_semaphore()
 
@@ -87,15 +93,12 @@
 
     lpad[...] = jnp.zeros_like(lpad)
     lg[...] = jnp.zeros_like(lg)
-    loads[0].wait()
-    loads[1].wait()
+    load_x.wait()
+    load_rw.wait()
     lpad[:, 0:12] = dot_nt(xin[...], rw[...])
     turned = lpad[...].T
     for head in range(4):
         lg[head, 0:HEADS, :] = turned[HEADS * head : HEADS * (head + 1)]
-    loads[2].wait()
-    loads[3].wait()
-
     pl.semaphore_wait(barrier, 12)
 
     logit_copies = []
@@ -105,6 +108,8 @@
         copy.start()
         logit_copies.append(copy)
 
+    for copy in load_kv:
+        copy.wait()
     halo = [
         remote(k.at[pl.ds(ROWS - HDIM, HDIM)], hk, hss.at[0], hrs.at[0], (tok + 1, z)),
         remote(v.at[pl.ds(ROWS - HDIM, HDIM)], hv, hss.at[1], hrs.at[1], (tok + 1, z)),
@@ -120,11 +125,10 @@
         hk[...] = jnp.zeros_like(hk)
         hv[...] = jnp.zeros_like(hv)
 
-    for load in loads[4:7]:
-        load.wait()
-
-    def before_rates(h, carry):
-        columns = pl.ds(pl.multiple_of(h * HDIM, HDIM), HDIM)
+    def before_rates(h):
+        for copy in load_w[h]:
+            copy.wait()
+        columns = pl.ds(h * HDIM, HDIM)
         first = w1[h].astype(BF16)
         third = w3[h].astype(BF16)
         second = w2[h].astype(BF16)
@@ -142,9 +146,9 @@
             pg[h, rows, :] = back * up * sig * (1.0 + gate * (1.0 - sig))
             pu[h, rows, :] = back * activ
             hd[h, rows, :] = -(activ * up)
-        return carry
-
-    lax.fori_loop(0, HEADS, before_rates, 0)
+
+    for h in range(HEADS):
+        before_rates(h)
 
     for copy in logit_copies:
         copy.wait_recv()
@@ -205,23 +209,25 @@
         for j, (left, right) in enumerate(wides):
             m = 3 * h + j
             scaled = (rate * right[h]).astype(BF16)
-            gs0[m] = dot(left[h, other, :], scaled).astype(BF16)
+            whole[m % 2] = dot(left[h], scaled)
+            gs0[m] = whole[m % 2, other, :].astype(BF16)
             s0[m].start()
-            gown[m] = dot(left[h, mine, :], scaled)
-            if m > 1:
-                send_chip_sum(m - 2)
-    send_chip_sum(MATS - 2)
-    send_chip_sum(MATS - 1)
-
+            gown[m] = whole[m % 2, mine, :]
+            if m >= LAG:
+                send_chip_sum(m - LAG)
+    for m in range(MATS - LAG, MATS):
+        send_chip_sum(m)
     for copy in every[0]:
         copy.wait_recv()
-    total = gown[0, quarter(x), :] + erx[0, 0].astype(F32) + erx[0, 1].astype(F32) + erx[0, 2].astype(F32)
+    total = gown[0, quarter(x), :]
+    for d in range(3):
+        total = total + erx[0, d].astype(F32)
     eq[...] = total
     es[...] = total.astype(BF16)
     for copy in every[1]:
         copy.start()
 
-    loads[7].wait()
+    load_q.wait()
 
     @pl.when(tok > 0)
     def _():
@@ -256,13 +262,6 @@
 
     lax.fori_loop(0, HEADS, attend, 0)
 
-    for copy in every[1]:
-        copy.wait_recv()
-    total = eq[...] + erx[1, 0].astype(F32) + erx[1, 1].astype(F32) + erx[1, 2].astype(F32)
-    gfull[2, my_quarter, :] = total.astype(BF16)
-    for copy in every[2]:
-        copy.start()
-
     owned = (2 * x + 1, 2 * y + 2)
     second_copies = [
         [
@@ -288,7 +287,7 @@
         remote(gfull.at[slot, mine], gfull.at[slot, mine], ssx.at[slot], rsx.at[slot], sibling) for slot in range(3)
     ]
 
-    for slot in range(2):
+    def first_sum(slot):
         m = owned[slot]
         total = gown[m]
         for d in range(3):
@@ -299,12 +298,7 @@
         for copy in second_copies[slot]:
             copy.start()
 
-    for d, x_there in ((d, lax.rem(x + 4 - d, 4)) for d in (2, 1, 3)):
-        theirs = quarter(c * 4 + x_there)
-        remote(gfull.at[2, theirs], gfull.at[2, theirs], ess.at[2, d - 1], ers.at[2, d - 1], sibling).wait_recv()
-    half_copies[2].start()
-
-    for slot in range(2):
+    def second_sum(slot):
         total = gown[owned[slot]]
         for copy in second_copies[slot]:
             copy.wait_recv()
@@ -313,49 +307,64 @@
         gfull[slot, mine, :] = total.astype(BF16)
         half_copies[slot].start()
 
-    for copy in half_copies:
+    def orthogonalize(slots):
+        iterates = []
+        for slot in slots:
+            half_copies[slot].wait_recv()
+            full = gfull[slot].astype(F32)
+            norm = jnp.sqrt(jnp.sum(full * full, keepdims=True)) + EPS_SCALE
+            iterates.append((full / norm).astype(BF16))
+        for repeat in range(STEPS):
+            grams = [dot_nt(it, it).astype(BF16) for it in iterates]
+            mixing = [
+                (COEF_B * gram.astype(F32) + COEF_C * dot(gram, gram)).astype(BF16) for gram in grams
+            ]
+            iterates = [
+                (COEF_A * it.astype(F32) + dot(mix, it)).astype(BF16) for mix, it in zip(mixing, iterates)
+            ]
+        for slot, it in zip(slots, iterates):
+            oall[0 if slot == 2 else owned[slot]] = it
+
+    first_sum(0)
+    first_sum(1)
+    for copy in every[1]:
         copy.wait_recv()
-
-    iterates = []
-    for slot in range(3):
-        full = gfull[slot].astype(F32)
-        norm = jnp.sqrt(jnp.sum(full * full, keepdims=True)) + EPS_SCALE
-        iterates.append((full / norm).astype(BF16))
-    for repeat in range(STEPS):
-        grams = [dot_nt(it, it).astype(BF16) for it in iterates]
-        mixing = [
-            (COEF_B * gram.astype(F32) + COEF_C * dot(gram, gram)).astype(BF16) for gram in grams
-        ]
-        iterates = [
-            (COEF_A * it.astype(F32) + dot(mix, it)).astype(BF16) for mix, it in zip(mixing, iterates)
-        ]
-
-    for slot in range(2):
-        oall[owned[slot]] = iterates[slot]
+    total = eq[...]
+    for d in range(3):
+        total = total + erx[1, d].astype(F32)
+    gfull[2, my_quarter, :] = total.astype(BF16)
+    for copy in every[2]:
+        copy.start()
+    second_sum(0)
+    second_sum(1)
+    orthogonalize([0, 1])
     for pair in zip(*third_copies):
         for copy in pair:
             copy.start()
-    oall[0] = iterates[2]
-
-    fourth_copies = [
-        remote(oall.at[m, mine], oall.at[m, mine], ss4.at[m], rs4.at[m], sibling) for m in range(MATS)
+    for d in (2, 1, 3):
+        theirs = quarter(c * 4 + lax.rem(x + 4 - d, 4))
+        remote(gfull.at[2, theirs], gfull.at[2, theirs], ess.at[2, d - 1], ers.at[2, d - 1], sibling).wait_recv()
+    half_copies[2].start()
+    orthogonalize([2])
+
+    fourth_copies = [None] + [
+        remote(oall.at[m, mine], oall.at[m, mine], ss4.at[m], rs4.at[m], sibling) for m in range(1, MATS)
     ]
 
     def foreign(m, action):
-        if m > 0:
-            axis, place = PLACE[m]
-            pl.when(where[axis] != place)(action)
-
-    def forward(m):
-        def action():
-            remote(oall.at[m, mine], oall.at[m, mine], ss4.at[m], rs3.at[m], sibling).wait_recv()
-            fourth_copies[m].start()
-
-        foreign(m, action)
+        axis, place = PLACE[m]
+        pl.when(where[axis] != place)(action)
+
+    def forward(d):
+        for m in (2 * lax.rem(x + d, 4) + 1, 2 * lax.rem(y + d, 4) + 2):
+            part = oall.at[m, mine]
+            remote(part, part, ss4.at[m], rs3.at[m], sibling).wait_recv()
+            remote(part, part, ss4.at[m], rs4.at[m], sibling).start()
 
     def apply(h):
         for j in range(3):
-            foreign(3 * h + j, fourth_copies[3 * h + j].wait_recv)
+            if 3 * h + j > 0:
+                foreign(3 * h + j, fourth_copies[3 * h + j].wait_recv)
         columns = pl.ds(h * HDIM, HDIM)
         size = scale_ref[h]
         first = (w1[h] - size * oall[3 * h].astype(F32)).astype(BF16)
@@ -373,8 +382,8 @@
             normed = fast * lax.rsqrt(spread + EPS_RMS) * gain
             out_ref[rows, columns] = (att[rows, columns] + normed).astype(BF16)
 
-    for m in range(1, MATS):
-        forward(m)
+    for d in (1, 3, 2):
+        forward(d)
     for h in range(HEADS):
         apply(h)
 
@@ -415,7 +424,7 @@
             pltpu.VMEM((HEADS, HDIM, FFN), F32),
             pltpu.VMEM((HEADS, HDIM, FFN), F32),
             pltpu.VMEM((HEADS, FFN, HDIM), F32),
-            dma((8,)),
+            dma((14,)),
             pltpu.VMEM((ROWS, 128), F32),
             pltpu.VMEM((4, 8, ROWS), F32),
             pltpu.VMEM((3, 8, ROWS), F32),
@@ -431,6 +440,7 @@
             pltpu.VMEM((HEADS, HDIM, ROWS), BF16),
             pltpu.VMEM((HEADS, HDIM, ROWS), BF16),
             pltpu.VMEM((ROWS, wide), F32),
+            pltpu.VMEM((2, HDIM, FFN), F32),
             pltpu.VMEM((QUARTER, FFN), F32),
             pltpu.VMEM((QUARTER, FFN), BF16),
             pltpu.VMEM((2, 3, QUARTER, FFN), BF16),

time: 55.6 us -> 54 us (0.971)
  Pallas kernels: 53.3 us -> 51.8 us
    pallas_call x1, Pallas kernels: 53.3 us -> 51.8 us  [on_device(): pl.pallas_call(kernel, name='layer', out_shape=jax.ShapeDtypeStruct((ROWS...]
where the time goes in v3:
time: 54 us; the launch traced here: 53.8 us
  Pallas kernels  51.8 us (96%)
  local copies, waits for them, and re-layouts  2.06 us (4%)
    pallas_call x1, Pallas kernels, on_device(): pl.pallas_call(kernel, name='layer', out_shape=jax.ShapeDtypeStruct((ROWS...  51.8 us
    unnamed x1, local copies, waits for them, and re-layouts  2.06 us

profile of v3, /device:TPU:1, one launch (start us, length us, event | category | flops | bytes accessed | tf_op | source)
XLA Modules:
  0.0 53.8 jit_solution(2343828423308010275)
XLA Ops:
  0.0 51.8 %layer.1 = bf16[512,768]{1,0:T(8,128)(2,1)} custom-call(bf16[512,1280]{1,0:T(8,128)(2,1)} %x_hbm.1, bf16[12,1280]{1,0:T(8,128)(2,1)} %bitcast.1, bf16[512,768]{1,0:T(8,128)(2,1)} %q_hbm.1, bf16[512,768]{1,0:T(8,128)(2,1)} %k_hbm.1, bf16[512,768]{1,0:T(8,128)(2,1)} %v_hbm.1, f32[3,256,512]{2,1,0:T(8,128)} %w1_hbm.1, f32[3,256,512]{2,1,0:T(8,128)} %w3_hbm.1, ...), custom_call_target="tpu_custom_call" | custom-call | tf_op jit(solution)/shard_map/layer/pallas_call | solution.py:411
  51.8 2.1 %copy.12 = bf16[512,768]{1,0:T(8,128)(2,1)} copy(bf16[512,768]{1,0:T(8,128)(2,1)} %layer.1) | data formatting | bytes 1572864

commit v4 on v3

--- a/solution.py
+++ b/solution.py
@@ -24,6 +24,9 @@
 PLACE = [None] + [((m - 1) % 2, (m - 1) // 2) for m in range(1, MATS)]
 QUARTER = HALF // 4
 LAG = 5
+SPLIT = 2
+PART = HALF // SPLIT
+PARTS = [pl.ds(i * PART, PART) for i in range(SPLIT)]
 
 
 def dot(a, b):
@@ -35,7 +38,8 @@
 
 
 def kernel(
-    x_hbm, rw_hbm, q_hbm, k_hbm, v_hbm, w1_hbm, w3_hbm, w2_hbm, scale_ref, gain_ref, out_ref,
+    x_hbm, rw_hbm, q_hbm, k_hbm, v_hbm, w1_hbm, w3_hbm, w2_hbm, scale_ref, gain_ref, out_hbm,
+    out_ref, out_sem,
     xin, rw, q, k, v, w1, w3, w2, load_sem,
     lpad, lg, lrx, lss, lrs,
     hk, hv, hss, hrs,
@@ -168,7 +172,13 @@
         step = lax.rem(place - where[axis] + 4, 4)
         index = jnp.maximum(step - 1, 0)
         s1.append(
-            remote(gs1.at[m], rx1.at[axis, index], ss1.at[m], rs1.at[axis, index], on_axis(axis, place))
+            [
+                remote(
+                    gs1.at[m, part], rx1.at[axis, index, part], ss1.at[m, i], rs1.at[axis, index, i],
+                    on_axis(axis, place),
+                )
+                for i, part in enumerate(PARTS)
+            ]
         )
 
     def quarter(place):
@@ -201,7 +211,8 @@
 
         @pl.when(where[axis] != place)
         def _():
-            s1[m].start()
+            for copy in s1[m]:
+                copy.start()
 
     for h in range(HEADS):
         rate = rates_down[:, h : h + 1]
@@ -266,51 +277,61 @@
     second_copies = [
         [
             remote(
-                gs2.at[slot], rx2.at[slot, d - 1], ss2.at[slot, d - 1], rs2.at[slot, d - 1],
+                gs2.at[slot, part], rx2.at[slot, d - 1, part], ss2.at[slot, d - 1, i], rs2.at[slot, d - 1, i],
                 on_axis(1 - slot, lax.rem(where[1 - slot] + d, 4)),
             )
+            for i, part in enumerate(PARTS)
             for d in (2, 1, 3)
         ]
         for slot in range(2)
     ]
+    def my_part(i):
+        return pl.ds(pl.multiple_of(c * HALF + i * PART, PART), PART)
+
     third_copies = [
         [
             remote(
-                oall.at[owned[slot], mine], oall.at[owned[slot], mine], ss3.at[slot, d - 1], rs3.at[owned[slot]],
-                on_axis(slot, lax.rem(where[slot] + d, 4)),
+                oall.at[owned[slot], my_part(i)], oall.at[owned[slot], my_part(i)],
+                ss3.at[slot, d - 1, i], rs3.at[owned[slot], i], on_axis(slot, lax.rem(where[slot] + d, 4)),
             )
+            for i in range(SPLIT)
             for d in (2, 1, 3)
         ]
         for slot in range(2)
     ]
     half_copies = [
-        remote(gfull.at[slot, mine], gfull.at[slot, mine], ssx.at[slot], rsx.at[slot], sibling) for slot in range(3)
-    ]
-
-    def first_sum(slot):
-        m = owned[slot]
-        total = gown[m]
+        [
+            remote(gfull.at[slot, my_part(i)], gfull.at[slot, my_part(i)], ssx.at[slot, i], rsx.at[slot, i], sibling)
+            for i in range(SPLIT)
+        ]
+        for slot in range(2)
+    ] + [[remote(gfull.at[2, mine], gfull.at[2, mine], ssx.at[2, 0], rsx.at[2, 0], sibling)]]
+
+    def first_sum(slot, i):
+        m, part = owned[slot], PARTS[i]
+        total = gown[m, part, :]
         for d in range(3):
-            remote(gs1.at[m], rx1.at[slot, d], ss1.at[m], rs1.at[slot, d], sibling).wait_recv()
-            total = total + rx1[slot, d].astype(F32)
-        gown[m] = total
-        gs2[slot] = total.astype(BF16)
-        for copy in second_copies[slot]:
+            remote(gs1.at[m, part], rx1.at[slot, d, part], ss1.at[m, i], rs1.at[slot, d, i], sibling).wait_recv()
+            total = total + rx1[slot, d, part, :].astype(F32)
+        gown[m, part, :] = total
+        gs2[slot, part, :] = total.astype(BF16)
+        for copy in second_copies[slot][3 * i : 3 * i + 3]:
             copy.start()
 
-    def second_sum(slot):
-        total = gown[owned[slot]]
-        for copy in second_copies[slot]:
+    def second_sum(slot, i):
+        total = gown[owned[slot], PARTS[i], :]
+        for copy in second_copies[slot][3 * i : 3 * i + 3]:
             copy.wait_recv()
         for d in range(3):
-            total = total + rx2[slot, d].astype(F32)
-        gfull[slot, mine, :] = total.astype(BF16)
-        half_copies[slot].start()
+            total = total + rx2[slot, d, PARTS[i], :].astype(F32)
+        gfull[slot, my_part(i), :] = total.astype(BF16)
+        half_copies[slot][i].start()
 
     def orthogonalize(slots):
         iterates = []
         for slot in slots:
-            half_copies[slot].wait_recv()
+            for copy in half_copies[slot]:
+                copy.wait_recv()
             full = gfull[slot].astype(F32)
             norm = jnp.sqrt(jnp.sum(full * full, keepdims=True)) + EPS_SCALE
             iterates.append((full / norm).astype(BF16))
@@ -325,8 +346,9 @@
         for slot, it in zip(slots, iterates):
             oall[0 if slot == 2 else owned[slot]] = it
 
-    first_sum(0)
-    first_sum(1)
+    for i in range(SPLIT):
+        first_sum(0, i)
+        first_sum(1, i)
     for copy in every[1]:
         copy.wait_recv()
     total = eq[...]
@@ -335,8 +357,9 @@
     gfull[2, my_quarter, :] = total.astype(BF16)
     for copy in every[2]:
         copy.start()
-    second_sum(0)
-    second_sum(1)
+    for i in range(SPLIT):
+        second_sum(0, i)
+        second_sum(1, i)
     orthogonalize([0, 1])
     for pair in zip(*third_copies):
         for copy in pair:
@@ -344,27 +367,32 @@
     for d in (2, 1, 3):
         theirs = quarter(c * 4 + lax.rem(x + 4 - d, 4))
         remote(gfull.at[2, theirs], gfull.at[2, theirs], ess.at[2, d - 1], ers.at[2, d - 1], sibling).wait_recv()
-    half_copies[2].start()
+    half_copies[2][0].start()
     orthogonalize([2])
 
     fourth_copies = [None] + [
-        remote(oall.at[m, mine], oall.at[m, mine], ss4.at[m], rs4.at[m], sibling) for m in range(1, MATS)
+        [
+            remote(oall.at[m, my_part(i)], oall.at[m, my_part(i)], ss4.at[m, i], rs4.at[m, i], sibling)
+            for i in range(SPLIT)
+        ]
+        for m in range(1, MATS)
     ]
 
     def foreign(m, action):
         axis, place = PLACE[m]
         pl.when(where[axis] != place)(action)
 
-    def forward(d):
+    def forward(d, i):
         for m in (2 * lax.rem(x + d, 4) + 1, 2 * lax.rem(y + d, 4) + 2):
-            part = oall.at[m, mine]
-            remote(part, part, ss4.at[m], rs3.at[m], sibling).wait_recv()
-            remote(part, part, ss4.at[m], rs4.at[m], sibling).start()
+            part = oall.at[m, my_part(i)]
+            remote(part, part, ss4.at[m, i], rs3.at[m, i], sibling).wait_recv()
+            remote(part, part, ss4.at[m, i], rs4.at[m, i], sibling).start()
 
     def apply(h):
         for j in range(3):
             if 3 * h + j > 0:
-                foreign(3 * h + j, fourth_copies[3 * h + j].wait_recv)
+                for copy in fourth_copies[3 * h + j]:
+                    foreign(3 * h + j, copy.wait_recv)
         columns = pl.ds(h * HDIM, HDIM)
         size = scale_ref[h]
         first = (w1[h] - size * oall[3 * h].astype(F32)).astype(BF16)
@@ -382,11 +410,19 @@
             normed = fast * lax.rsqrt(spread + EPS_RMS) * gain
             out_ref[rows, columns] = (att[rows, columns] + normed).astype(BF16)
 
-    for d in (1, 3, 2):
-        forward(d)
+    for i in range(SPLIT):
+        for d in (1, 3, 2):
+            forward(d, i)
+    out_copies = []
     for h in range(HEADS):
         apply(h)
-
+        columns = pl.ds(h * HDIM, HDIM)
+        copy = pltpu.make_async_copy(out_ref.at[:, columns], out_hbm.at[:, columns], out_sem.at[h])
+        copy.start()
+        out_copies.append(copy)
+
+    for copy in out_copies:
+        copy.wait()
     for copy in logit_copies + s0:
         copy.wait_send()
 
@@ -396,9 +432,9 @@
             copy.wait_send()
 
     for m in range(1, MATS):
-        foreign(m, s1[m].wait_send)
-        foreign(m, fourth_copies[m].wait_send)
-    for copies in every + second_copies + [half_copies] + third_copies:
+        for copy in s1[m] + fourth_copies[m]:
+            foreign(m, copy.wait_send)
+    for copies in every + second_copies + half_copies + third_copies:
         for copy in copies:
             copy.wait_send()
 
@@ -414,8 +450,10 @@
         out_shape=jax.ShapeDtypeStruct((ROWS, wide), BF16),
         in_specs=[anywhere] * 8
         + [pl.BlockSpec(memory_space=pltpu.SMEM), pl.BlockSpec(memory_space=pltpu.VMEM)],
-        out_specs=pl.BlockSpec(memory_space=pltpu.VMEM),
+        out_specs=anywhere,
         scratch_shapes=[
+            pltpu.VMEM((ROWS, wide), BF16),
+            dma((HEADS,)),
             pltpu.VMEM((ROWS, features), BF16),
             pltpu.VMEM((rw.shape[1], rw.shape[0]), BF16),
             pltpu.VMEM((ROWS, wide), BF16),
@@ -457,16 +495,16 @@
             pltpu.VMEM((MATS, HDIM, FFN), BF16),
             dma((MATS,)),
             dma((MATS,)),
-            dma((MATS,)),
-            dma((2, 3)),
-            dma((2, 3)),
-            dma((2, 3)),
-            dma((3,)),
-            dma((3,)),
-            dma((2, 3)),
-            dma((MATS,)),
-            dma((MATS,)),
-            dma((MATS,)),
+            dma((MATS, SPLIT)),
+            dma((2, 3, SPLIT)),
+            dma((2, 3, SPLIT)),
+            dma((2, 3, SPLIT)),
+            dma((3, SPLIT)),
+            dma((3, SPLIT)),
+            dma((2, 3, SPLIT)),
+            dma((MATS, SPLIT)),
+            dma((MATS, SPLIT)),
+            dma((MATS, SPLIT)),
         ],
         compiler_params=pltpu.CompilerParams(
             collective_id=0, has_side_effects=True, vmem_limit_bytes=56 << 20

time: 54 us -> 52.6 us (0.974)
  Pallas kernels: 51.8 us -> 50.3 us
    pallas_call x1, Pallas kernels: 51.8 us -> 50.3 us  [on_device(): pl.pallas_call(kernel, name='layer', out_shape=jax.ShapeDtypeStruct((ROWS...]
where the time goes in v4:
time: 52.6 us; the launch traced here: 52.4 us
  Pallas kernels  50.3 us (96%)
  local copies, waits for them, and re-layouts  2.06 us (4%)
    pallas_call x1, Pallas kernels, on_device(): pl.pallas_call(kernel, name='layer', out_shape=jax.ShapeDtypeStruct((ROWS...  50.3 us
    unnamed x1, local copies, waits for them, and re-layouts  2.06 us

profile of v4, /device:TPU:1, one launch (start us, length us, event | category | flops | bytes accessed | tf_op | source)
XLA Modules:
  0.0 52.4 jit_solution(1774944395098763422)
XLA Ops:
  0.0 50.3 %layer.1 = bf16[512,768]{1,0:T(8,128)(2,1)} custom-call(bf16[512,1280]{1,0:T(8,128)(2,1)} %x_hbm.1, bf16[12,1280]{1,0:T(8,128)(2,1)} %bitcast.1, bf16[512,768]{1,0:T(8,128)(2,1)} %q_hbm.1, bf16[512,768]{1,0:T(8,128)(2,1)} %k_hbm.1, bf16[512,768]{1,0:T(8,128)(2,1)} %v_hbm.1, f32[3,256,512]{2,1,0:T(8,128)} %w1_hbm.1, f32[3,256,512]{2,1,0:T(8,128)} %w3_hbm.1, ...), custom_call_target="tpu_custom_call" | custom-call | tf_op jit(solution)/shard_map/layer/pallas_call | solution.py:447
  50.3 2.1 %copy.12 = bf16[512,768]{1,0:T(8,128)(2,1)} copy(bf16[512,768]{1,0:T(8,128)(2,1)} %layer.1) | data formatting | bytes 1572864

commit v5 on v4

--- a/solution.py
+++ b/solution.py
@@ -23,7 +23,7 @@
 
 PLACE = [None] + [((m - 1) % 2, (m - 1) // 2) for m in range(1, MATS)]
 QUARTER = HALF // 4
-LAG = 5
+LAG = 4
 SPLIT = 2
 PART = HALF // SPLIT
 PARTS = [pl.ds(i * PART, PART) for i in range(SPLIT)]

time: 52.6 us -> 53 us (level)
  no operation moved by 1% of the time
where the time goes in v5:
time: 53 us; the launch traced here: 52.8 us
  Pallas kernels  50.7 us (96%)
  local copies, waits for them, and re-layouts  2.06 us (4%)
    pallas_call x1, Pallas kernels, on_device(): pl.pallas_call(kernel, name='layer', out_shape=jax.ShapeDtypeStruct((ROWS...  50.7 us
    unnamed x1, local copies, waits for them, and re-layouts  2.06 us

profile of v5, /device:TPU:1, one launch (start us, length us, event | category | flops | bytes accessed | tf_op | source)
XLA Modules:
  0.0 52.8 jit_solution(18308129165658430595)
XLA Ops:
  0.0 50.7 %layer.1 = bf16[512,768]{1,0:T(8,128)(2,1)} custom-call(bf16[512,1280]{1,0:T(8,128)(2,1)} %x_hbm.1, bf16[12,1280]{1,0:T(8,128)(2,1)} %bitcast.1, bf16[512,768]{1,0:T(8,128)(2,1)} %q_hbm.1, bf16[512,768]{1,0:T(8,128)(2,1)} %k_hbm.1, bf16[512,768]{1,0:T(8,128)(2,1)} %v_hbm.1, f32[3,256,512]{2,1,0:T(8,128)} %w1_hbm.1, f32[3,256,512]{2,1,0:T(8,128)} %w3_hbm.1, ...), custom_call_target="tpu_custom_call" | custom-call | tf_op jit(solution)/shard_map/layer/pallas_call | solution.py:447
  50.7 2.1 %copy.12 = bf16[512,768]{1,0:T(8,128)(2,1)} copy(bf16[512,768]{1,0:T(8,128)(2,1)} %layer.1) | data formatting | bytes 1572864
